TPU v7x, 32 devices: a whole 2x2x4 slice. The times are simulated.
32 devices in a mesh: row: 4 (over y, x), col: 8 (over z, core).
Axes of the slice: x: 2, y: 2, z: 4, core: 2. Of those that a mesh axis runs over, the one named last changes fastest.
Arguments:
- tokens: bfloat16 [512, 5120], P('row'), may hold values from -6 to 6
- expert_ids: int32 [512], replicated, may hold values from 0 to 7
- modality: int32 [512], replicated, may hold values from 0 to 1
- tile_counts: int32 [2, 8], replicated, may hold values from 1 to 4, as said below
- router: bfloat16 [5120, 8], P(None, 'col'), may hold values from -0.15625 to 0.15625
- w_gate: bfloat16 [8, 5120, 4096], P('col', None, 'row'), may hold values from -0.078125 to 0.078125
- w_up: bfloat16 [8, 5120, 4096], P('col', None, 'row'), may hold values from -0.078125 to 0.078125
- w_down: bfloat16 [8, 4096, 5120], P('col', 'row'), may hold values from -0.09375 to 0.09375
- shared_gate: bfloat16 [5120, 8192], P('row', 'col'), may hold values from -0.078125 to 0.078125
- shared_up: bfloat16 [5120, 8192], P('row', 'col'), may hold values from -0.078125 to 0.078125
- shared_down: bfloat16 [8192, 5120], P('col', 'row'), may hold values from -0.0625 to 0.0625
Outputs:
- mixed: bfloat16 [512, 5120], P('col', 'row')
Inputs may be any that keep to these rules, and one draw needn't show every extreme that they name: `tile_counts`: in every draw some expert's text segment has 4 tiles and at least 32 text tokens, and some expert's image segment has 4 tiles and at least 32 image tokens.
All inputs are finite; a program needn't handle non-finite values.
Results may differ from a plain program's by a relative error of at most 0.0052.
Values may be sent and summed in bfloat16 or wider, within the bound.
No kernel may reach another device: no remote copies, remote signals or barrier semaphores. Data moves between devices by JAX's collectives and lax.ppermute only.
A program may use at most 128 MiB of HBM per device.

v0:
```python
import functools

import jax
import jax.numpy as jnp
from jax import lax
from jax.experimental import pallas as pl
from jax.experimental.pallas import tpu as pltpu
from jax.sharding import PartitionSpec as P

TILE = 8
MAXT = 4


def table_kernel(n_row, half, where, counts, ids_ref, kinds_ref, in_ref, out_ref):
    row, col = where[0], where[1]
    count = ids_ref.shape[1]
    capacity = MAXT * TILE
    at = lax.broadcasted_iota(jnp.int32, (1, count), 1)
    index = at // half
    before = lax.broadcasted_iota(jnp.int32, (count, count), 0)
    ids, kinds = ids_ref[...], kinds_ref[...]
    members = []
    for kind in range(2):
        member = jnp.where((ids == col) & (kinds == kind), 1.0, 0.0)
        members.append(jnp.broadcast_to(member, (8, count)).astype(jnp.bfloat16))
    for base, table_ref in ((row, in_ref), (col >> 1, out_ref)):
        chunk = (base ^ (index % n_row)) * 2 + ((col & 1) ^ (index // n_row))
        token = chunk * half + at % half
        earlier = jnp.where(before < token, 1.0, 0.0).astype(jnp.bfloat16)
        same = jnp.where(before == token, 1.0, 0.0).astype(jnp.bfloat16)
        places = jnp.full((1, count), -1, jnp.int32)
        for kind in range(2):
            rank = jnp.dot(members[kind], earlier, preferred_element_type=jnp.float32)[:1]
            here = jnp.dot(members[kind], same, preferred_element_type=jnp.float32)[:1]
            rank = rank.astype(jnp.int32)
            keep = (here > 0.5) & (rank < counts[kind, col] * TILE)
            places = jnp.where(keep, kind * capacity + rank, places)
        slots = lax.broadcasted_iota(jnp.int32, (2 * capacity, count), 0)
        table = jnp.where(slots == places, 1.0, 0.0).astype(jnp.bfloat16)
        for start in range(0, table_ref.shape[0], 2 * capacity):
            table_ref[pl.ds(start, 2 * capacity), :] = table


def slot_tables(expert_ids, modality, tile_counts, row, col, n_row, half):
    count = expert_ids.shape[0]
    slots = 2 * MAXT * TILE
    smem = pl.BlockSpec(memory_space=pltpu.SMEM)
    vmem = pl.BlockSpec(memory_space=pltpu.VMEM)
    return pl.pallas_call(
        functools.partial(table_kernel, n_row, half),
        out_shape=[
            jax.ShapeDtypeStruct((slots, count), jnp.bfloat16),
            jax.ShapeDtypeStruct((2 * slots, count), jnp.bfloat16),
        ],
        in_specs=[smem, smem, vmem, vmem],
        out_specs=[vmem, vmem],
        name="slot_tables",
        cost_estimate=pl.CostEstimate(
            flops=64 * count * count, bytes_accessed=8 * count, transcendentals=0
        ),
    )(jnp.stack([row, col]), tile_counts, expert_ids[None], modality[None])


def expert_kernel(x_ref, gate_hbm, up_hbm, down_hbm, out_ref, ring, down, gate_sum, up_sum, sems):
    steps = sems.shape[1]
    slots, depth = ring.shape[1], ring.shape[2]
    wide = down.shape[2]
    loads = []
    for i in range(steps):
        rows = pl.ds(i * depth, depth)
        loads.append(
            [
                pltpu.make_async_copy(hbm.at[0, rows], ring.at[k, i % slots], sems.at[k, i])
                for k, hbm in enumerate((gate_hbm, up_hbm))
            ]
        )
    for i in range(steps):
        columns = pl.ds(i * wide, wide)
        loads.append([pltpu.make_async_copy(down_hbm.at[0, :, columns], down.at[i], sems.at[2, i])])

    def start(i):
        for load in loads[i]:
            load.start()

    for i in range(slots):
        start(i)
    for i in range(steps):
        x = x_ref[:, pl.ds(i * depth, depth)]
        for k, total in enumerate((gate_sum, up_sum)):
            loads[i][k].wait()
            part = jnp.dot(x, ring[k, i % slots], preferred_element_type=jnp.float32)
            total[...] = part if i == 0 else total[...] + part
        if i + slots < steps:
            start(i + slots)
        else:
            first = steps + 2 * (i + slots - steps)
            for j in range(first, min(first + 2, 2 * steps)):
                start(j)
    for j in range(steps + 2 * slots, 2 * steps):
        start(j)
    value = gate_sum[...]
    hidden = (value / (1.0 + jnp.exp(-value)) * up_sum[...]).astype(jnp.bfloat16)
    for i in range(steps):
        loads[steps + i][0].wait()
        columns = pl.ds(i * wide, wide)
        out_ref[:, columns] = jnp.dot(hidden, down[i], preferred_element_type=jnp.float32)


def expert(scaled, w_gate, w_up, w_down):
    slots, model = scaled.shape
    units = w_gate.shape[2]
    steps = 5
    assert model % (steps * 128) == 0
    vmem = pl.BlockSpec(memory_space=pltpu.VMEM)
    whole = pl.BlockSpec(memory_space=pl.ANY)
    return pl.pallas_call(
        expert_kernel,
        out_shape=jax.ShapeDtypeStruct((slots, model), jnp.float32),
        in_specs=[vmem, whole, whole, whole],
        out_specs=vmem,
        scratch_shapes=[
            pltpu.VMEM((2, 3, model // steps, units), jnp.bfloat16),
            pltpu.VMEM((steps, units, model // steps), jnp.bfloat16),
            pltpu.VMEM((slots, units), jnp.float32),
            pltpu.VMEM((slots, units), jnp.float32),
            pltpu.SemaphoreType.DMA((3, steps)),
        ],
        name="routed_expert",
        compiler_params=pltpu.CompilerParams(vmem_limit_bytes=29 * 2**20),
        cost_estimate=pl.CostEstimate(
            flops=6 * slots * model * units,
            bytes_accessed=6 * model * units,
            transcendentals=slots * units,
        ),
    )(scaled, w_gate, w_up, w_down)


def swap(values, axis, step):
    size = lax.axis_size(axis)
    return lax.ppermute(values, axis, [(i, i ^ step) for i in range(size)])


def bit_half(values, axis, bit, value):
    shape = values.shape
    n = shape[axis]
    low = 2**bit
    split = shape[:axis] + (n // (2 * low), 2, low) + shape[axis + 1 :]
    part = lax.index_in_dim(values.reshape(split), value, axis + 1, keepdims=False)
    return part.reshape(shape[:axis] + (n // 2,) + shape[axis + 1 :])


def bit_join(first, second, axis, bit):
    shape = first.shape
    n = shape[axis]
    low = 2**bit
    split = shape[:axis] + (n // low, 1, low) + shape[axis + 1 :]
    both = jnp.concatenate([first.reshape(split), second.reshape(split)], axis=axis + 1)
    return both.reshape(shape[:axis] + (2 * n,) + shape[axis + 1 :])


def halve_first(local, weight, bit):
    def dot(rows):
        flat = rows.reshape(-1, rows.shape[-1])
        out = jnp.dot(flat, weight, preferred_element_type=jnp.float32)
        return out.reshape(rows.shape[:-1] + (weight.shape[1],))

    away = dot(bit_half(local, 1, bit, 1)).astype(jnp.bfloat16)
    came = swap(away, "row", 2**bit)
    kept = dot(bit_half(local, 1, bit, 0))
    return lax.optimization_barrier(kept), came


def halve_rest(kept, came, order):
    total = kept + came.astype(jnp.float32)
    done = [order[0]]
    for bit in order[1:]:
        at = bit - sum(1 for d in done if d < bit)
        away = bit_half(total, 1, at, 1).astype(jnp.bfloat16)
        came = swap(away, "row", 2**bit)
        total = bit_half(total, 1, at, 0) + came.astype(jnp.float32)
        done.append(bit)
    return total


def spread(values, order):
    done = []
    for bit in order:
        came = swap(values, "row", 2**bit)
        at = sum(1 for d in done if d < bit)
        values = bit_join(values, came, 1, at)
        done.append(bit)
    return values


def per_device(
    tokens,
    expert_ids,
    modality,
    tile_counts,
    router,
    w_gate,
    w_up,
    w_down,
    shared_gate,
    shared_up,
    shared_down,
):
    n_row, n_col = lax.axis_size("row"), lax.axis_size("col")
    bits = n_row.bit_length() - 1
    assert n_row == 2**bits and n_col == 2 * n_row
    row, col = lax.axis_index("row"), lax.axis_index("col")
    chip = col >> 1
    half = tokens.shape[0] // 2
    width = shared_down.shape[1]
    model = tokens.shape[1]

    def piece(block, top, source):
        return lax.dynamic_slice(source, (top, block * width), (half, width))

    mine, other = (col & 1) * half, (1 - (col & 1)) * half
    sent = [piece(row ^ s, mine, tokens) for s in range(1, n_row)]
    again, *sent = lax.optimization_barrier((tokens, *sent))
    fetched = [swap(part, "row", s + 1) for s, part in enumerate(sent)]
    crossed = [swap(f, "col", 1) for f in fetched]
    near = jnp.stack([piece(row, mine, again)] + fetched)
    far = jnp.stack([piece(row, other, again)] + crossed)
    local = jnp.stack([near, far])
    table, placing = slot_tables(expert_ids, modality, tile_counts, row, col, n_row, half)

    flat = local.reshape(-1, width)
    taken_part = jnp.dot(table, flat, preferred_element_type=jnp.float32).astype(jnp.bfloat16)
    taken = jnp.zeros((taken_part.shape[0], model), jnp.bfloat16)
    taken = lax.dynamic_update_slice(taken, taken_part, (0, row * width))
    for s in range(1, n_row):
        came = swap(taken_part, "row", s)
        taken = lax.dynamic_update_slice(taken, came, (0, (row ^ s) * width))

    upward, downward = list(range(bits)), list(range(bits))[::-1]
    gate_kept, gate_came = halve_first(local, shared_gate, upward[0])
    up_kept, up_came = halve_first(local, shared_up, downward[0])

    score = jax.nn.sigmoid(jnp.dot(taken, router, preferred_element_type=jnp.float32))
    scaled = (taken.astype(jnp.float32) * score).astype(jnp.bfloat16)
    result = expert(scaled, w_gate, w_up, w_down)
    gate_came, up_came, result = lax.optimization_barrier((gate_came, up_came, result))
    gate_sum = halve_rest(gate_kept, gate_came, upward)
    up_sum = halve_rest(up_kept, up_came, downward)

    def columns(block):
        return lax.dynamic_slice_in_dim(result, block * width, width, 1)

    slot_total = columns(row)
    for s in range(1, n_row):
        leaving = columns(row ^ s).astype(jnp.bfloat16)
        came = swap(leaving, "row", s)
        slot_total = slot_total + came.astype(jnp.float32)

    shared_hidden = (jax.nn.silu(gate_sum) * up_sum).astype(jnp.bfloat16)
    units = shared_hidden.shape[-1]
    first = spread(shared_hidden[..., : units // 2], downward)
    second = spread(shared_hidden[..., units // 2 :], upward)
    whole = jnp.concatenate([first, second], axis=-1)
    ordered = [lax.dynamic_index_in_dim(whole, row ^ chip ^ u, 1, False) for u in range(n_row)]
    outgoing = jnp.stack(ordered, axis=1).reshape(-1, units)

    high = slot_total.astype(jnp.bfloat16)
    low = (slot_total - high.astype(jnp.float32)).astype(jnp.bfloat16)
    pair = jnp.concatenate([high, low])
    split = outgoing.shape[0] // 2

    lanes = width // 2

    def combined(start, left):
        rows = outgoing[start : start + split]
        down = shared_down[:, left : left + lanes]
        part = jnp.dot(rows, down, preferred_element_type=jnp.float32)
        put = placing[:, start : start + split]
        return part + lax.dot_general(
            put,
            pair[:, left : left + lanes],
            (((0,), (0,)), ((), ())),
            preferred_element_type=jnp.float32,
        )

    streams = []
    for left in (0, lanes):
        came = swap(combined(split, left).astype(jnp.bfloat16), "col", 1)
        kept = lax.optimization_barrier(combined(0, left))
        total = (kept + came.astype(jnp.float32)).reshape(n_row, half, lanes)
        streams.append([total[u] for u in range(n_row)])
    for bit in range(bits):
        for i, blocks in enumerate(streams):
            away = jnp.stack(blocks[1::2]).astype(jnp.bfloat16)
            came = swap(away, "col", 2 ** (bit + 1))
            streams[i] = [b + came[j].astype(jnp.float32) for j, b in enumerate(blocks[0::2])]
    return jnp.concatenate([blocks[0] for blocks in streams], axis=1).astype(jnp.bfloat16)


def solution(mesh):
    in_specs = (
        P("row", None),
        P(),
        P(),
        P(),
        P(None, "col"),
        P("col", None, "row"),
        P("col", None, "row"),
        P("col", "row", None),
        P("row", "col"),
        P("row", "col"),
        P("col", "row"),
    )
    out_specs = P("col", "row")
    return jax.shard_map(
        per_device, mesh=mesh, in_specs=in_specs, out_specs=out_specs, check_vma=False
    )
```

profile of v0, /device:TPU:0, one launch (start us, length us, event | category | flops | bytes accessed | tf_op | source)
XLA Modules:
  0.0 91.8 jit_solution(4534352004387073577)
XLA Ops:
  0.0 1.9 %fusion.80 = (bf16[64,1280]{1,0:T(8,128)(2,1)S(1)}, bf16[64,1280]{1,0:T(8,128)(2,1)S(1)}, bf16[64,1280]{1,0:T(8,128)(2,1)}) fusion(bf16[128,5120]{1,0:T(8,128)(2,1)} %param.11, s32[]{:T(128)S(6)} %select_n.43, s32[]{:T(128)S(6)} %select_n.46, s32[]{:T(128)S(6)} %select_n.45, s32[]{:T(128)S(6)} %select_n.44), kind=kLoop, calls=%fused_computation.138 | loop fusion | bytes 983056 | tf_op jit(solution)/shard_map/dynamic_slice | solution.py:218
  1.9 3.0 %collective-permute-start = (bf16[64,1280]{1,0:T(8,128)(2,1)}, bf16[64,1280]{1,0:T(8,128)(2,1)S(1)}, u32[]{:S(2)}, u32[]{:S(2)}) collective-permute-start(bf16[64,1280]{1,0:T(8,128)(2,1)} %get-tuple-element.15), channel_id=1, source_target_pairs={{0,8},{8,0},{16,24},{24,16},{1,9},{9,1},{17,25},{25,17},{2,10},{10... | collective-permute-start | bytes 491528 | tf_op jit(solution)/shard_map/ppermute | solution.py:140
  4.9 1.5 %collective-permute-start.1 = (bf16[64,1280]{1,0:T(8,128)(2,1)S(1)}, bf16[64,1280]{1,0:T(8,128)(2,1)S(1)}, u32[]{:S(2)}, u32[]{:S(2)}) collective-permute-start(bf16[64,1280]{1,0:T(8,128)(2,1)S(1)} %get-tuple-element.16), channel_id=1, source_target_pairs={{0,16},{8,24},{16,0},{24,8},{1,17},{9,25},{17,1},{25,9},{2,18},{10... | collective-permute-start | bytes 491528 | tf_op jit(solution)/shard_map/ppermute | solution.py:140
  7.1 2.3 %slot_tables.1 = (bf16[64,512]{1,0:T(8,128)(2,1)}, bf16[128,512]{1,0:T(8,128)(2,1)}) custom-call(s32[2]{0:T(128)} %pad_add_fusion.where, s32[2,8]{1,0:T(2,128)} %counts.1, s32[1,512]{1,0:T(1,128)} %bitcast.185, s32[1,512]{1,0:T(1,128)} %bitcast.186), custom_call_target="tpu_custom_call" | custom-call | flops 16777216 | bytes 4096 | tf_op jit(solution)/shard_map/slot_tables/pallas_call | solution.py:49
  10.5 2.6 %collective-permute-done.1 = bf16[64,1280]{1,0:T(8,128)(2,1)S(1)} collective-permute-done((bf16[64,1280]{1,0:T(8,128)(2,1)S(1)}, bf16[64,1280]{1,0:T(8,128)(2,1)S(1)}, u32[]{:S(2)}, u32[]{:S(2)}) %collective-permute-start.1) | collective-permute-done | bytes 163872 | tf_op jit(solution)/shard_map/ppermute | solution.py:140
  16.8 1.5 %collective-permute-start.8 = (bf16[64,1280]{1,0:T(8,128)(2,1)S(1)}, bf16[64,1280]{1,0:T(8,128)(2,1)S(1)}, u32[]{:S(2)}, u32[]{:S(2)}) collective-permute-start(bf16[64,1280]{1,0:T(8,128)(2,1)S(1)} %get-tuple-element.60), channel_id=1, source_target_pairs={{0,8},{8,0},{16,24},{24,16},{1,9},{9,1},{17,25},{25,17},{2,10},{10... | collective-permute-start | bytes 491528 | tf_op jit(solution)/shard_map/ppermute | solution.py:140
  23.0 1.8 %collective-permute-start.7 = (bf16[2,2,64,1024]{3,2,0,1:T(8,128)(2,1)S(1)}, bf16[2,2,64,1024]{3,2,0,1:T(8,128)(2,1)S(1)}, u32[]{:S(2)}, u32[]{:S(2)}) collective-permute-start(bf16[2,2,64,1024]{3,2,0,1:T(8,128)(2,1)S(1)} %fusion.11), channel_id=1, source_target_pairs={{0,16},{8,24},{16,0},{24,8},{1,17},{9,25},{17,1},{25,9},{2,18},{10... | collective-permute-start | bytes 1572872 | tf_op jit(solution)/shard_map/ppermute | solution.py:140
  26.4 2.3 %collective-permute-done.10 = bf16[64,1280]{1,0:T(8,128)(2,1)S(1)} collective-permute-done((bf16[64,1280]{1,0:T(8,128)(2,1)S(1)}, bf16[64,1280]{1,0:T(8,128)(2,1)S(1)}, u32[]{:S(2)}, u32[]{:S(2)}) %collective-permute-start.10) | collective-permute-done | bytes 163872 | tf_op jit(solution)/shard_map/ppermute | solution.py:140
  29.2 8.4 %routed_expert.1 = f32[64,5120]{1,0:T(8,128)S(1)} custom-call(bf16[64,5120]{1,0:T(8,128)(2,1)S(1)} %multiply_convert_fusion.x_ref, bf16[1,5120,1024]{2,1,0:T(8,128)(2,1)S(1)} %bitcast.160, bf16[1,5120,1024]{2,1,0:T(8,128)(2,1)S(1)} %copy-done.2, bf16[1,1024,5120]{2,1,0:T(8,128)(2,1)} %down_hbm.1), custom_call_target="tpu_custom_call" | custom-call | flops 2013265920 | bytes 31457280 | tf_op jit(solution)/shard_map/routed_expert/pallas_call | solution.py:116
  37.6 1.6 %collective-permute-done.7 = bf16[2,2,64,1024]{3,2,0,1:T(8,128)(2,1)S(1)} collective-permute-done((bf16[2,2,64,1024]{3,2,0,1:T(8,128)(2,1)S(1)}, bf16[2,2,64,1024]{3,2,0,1:T(8,128)(2,1)S(1)}, u32[]{:S(2)}, u32[]{:S(2)}) %collective-permute-start.7) | collective-permute-done | bytes 524320 | tf_op jit(solution)/shard_map/ppermute | solution.py:140
  39.9 1.7 %collective-permute-start.18 = (bf16[64,1280]{1,0:T(8,128)(2,1)S(1)}, bf16[64,1280]{1,0:T(8,128)(2,1)S(1)}, u32[]{:S(2)}, u32[]{:S(2)}) collective-permute-start(bf16[64,1280]{1,0:T(8,128)(2,1)S(1)} %get-tuple-element.31), channel_id=1, source_target_pairs={{0,16},{8,24},{16,0},{24,8},{1,17},{9,25},{17,1},{25,9},{2,18},{10... | collective-permute-start | bytes 491528 | tf_op jit(solution)/shard_map/ppermute | solution.py:140
  43.8 1.7 %collective-permute-start.12 = (bf16[2,1,64,1024]{3,2,0,1:T(8,128)(2,1)S(1)}, bf16[2,1,64,1024]{3,2,0,1:T(8,128)(2,1)S(1)}, u32[]{:S(2)}, u32[]{:S(2)}) collective-permute-start(bf16[2,1,64,1024]{3,2,0,1:T(8,128)(2,1)S(1)} %fusion.42), channel_id=1, source_target_pairs={{0,8},{8,0},{16,24},{24,16},{1,9},{9,1},{17,25},{25,17},{2,10},{10... | collective-permute-start | bytes 786440 | tf_op jit(solution)/shard_map/ppermute | solution.py:140
  46.4 4.0 %collective-permute-done.18 = bf16[64,1280]{1,0:T(8,128)(2,1)S(1)} collective-permute-done((bf16[64,1280]{1,0:T(8,128)(2,1)S(1)}, bf16[64,1280]{1,0:T(8,128)(2,1)S(1)}, u32[]{:S(2)}, u32[]{:S(2)}) %collective-permute-start.18) | collective-permute-done | bytes 163872 | tf_op jit(solution)/shard_map/ppermute | solution.py:140
  51.0 3.7 %collective-permute-done.11 = bf16[2,1,64,1024]{3,2,0,1:T(8,128)(2,1)S(1)} collective-permute-done((bf16[2,1,64,1024]{3,2,0,1:T(8,128)(2,1)S(1)}, bf16[2,1,64,1024]{3,2,0,1:T(8,128)(2,1)S(1)}, u32[]{:S(2)}, u32[]{:S(2)}) %collective-permute-start.11) | collective-permute-done | bytes 262176 | tf_op jit(solution)/shard_map/ppermute | solution.py:140
  55.0 1.6 %collective-permute-start.15 = (bf16[2,1,64,512]{3,2,0,1:T(8,128)(2,1)S(1)}, bf16[2,1,64,512]{3,2,0,1:T(8,128)(2,1)S(1)}, u32[]{:S(2)}, u32[]{:S(2)}) collective-permute-start(bf16[2,1,64,512]{3,2,0,1:T(8,128)(2,1)S(1)} %get-tuple-element.55), channel_id=1, source_target_pairs={{0,8},{8,0},{16,24},{24,16},{1,9},{9,1},{17,25},{25,17},{2,10},{10... | collective-permute-start | bytes 393224 | tf_op jit(solution)/shard_map/ppermute | solution.py:140
  57.2 4.3 %collective-permute-done.13 = bf16[2,1,64,512]{3,2,0,1:T(8,128)(2,1)S(1)} collective-permute-done((bf16[2,1,64,512]{3,2,0,1:T(8,128)(2,1)S(1)}, bf16[2,1,64,512]{3,2,0,1:T(8,128)(2,1)S(1)}, u32[]{:S(2)}, u32[]{:S(2)}) %collective-permute-start.13) | collective-permute-done | bytes 131104 | tf_op jit(solution)/shard_map/ppermute | solution.py:140
  63.8 4.2 %collective-permute-done.14 = bf16[2,2,64,512]{3,2,0,1:T(8,128)(2,1)S(1)} collective-permute-done((bf16[2,2,64,512]{3,2,0,1:T(8,128)(2,1)S(1)}, bf16[2,2,64,512]{3,2,0,1:T(8,128)(2,1)S(1)}, u32[]{:S(2)}, u32[]{:S(2)}) %collective-permute-start.14) | collective-permute-done | bytes 262176 | tf_op jit(solution)/shard_map/ppermute | solution.py:140
  69.1 1.5 %copy-done.4 = bf16[1024,1280]{1,0:T(8,128)(2,1)S(1)} copy-done((bf16[1024,1280]{1,0:T(8,128)(2,1)S(1)}, bf16[1024,1280]{1,0:T(8,128)(2,1)}, u32[]{:S(2)}) %copy-start.4) | copy-done | bytes 2621464
  73.7 1.6 %collective-permute-start.21 = (bf16[2,64,640]{2,1,0:T(8,128)(2,1)S(1)}, bf16[2,64,640]{2,1,0:T(8,128)(2,1)S(1)}, u32[]{:S(2)}, u32[]{:S(2)}) collective-permute-start(bf16[2,64,640]{2,1,0:T(8,128)(2,1)S(1)} %pad_maximum_fusion.11), channel_id=1, source_target_pairs={{0,2},{1,3},{2,0},{3,1},{4,6},{5,7},{6,4},{7,5},{8,10},{9,11},{10,... | collective-permute-start | bytes 491528 | tf_op jit(solution)/shard_map/ppermute | solution.py:140
  76.0 4.8 %collective-permute-done.21 = bf16[2,64,640]{2,1,0:T(8,128)(2,1)S(1)} collective-permute-done((bf16[2,64,640]{2,1,0:T(8,128)(2,1)S(1)}, bf16[2,64,640]{2,1,0:T(8,128)(2,1)S(1)}, u32[]{:S(2)}, u32[]{:S(2)}) %collective-permute-start.21) | collective-permute-done | bytes 163872 | tf_op jit(solution)/shard_map/ppermute | solution.py:140
  80.9 2.7 %collective-permute-start.22 = (bf16[1,64,640]{2,1,0:T(8,128)(2,1)S(1)}, bf16[1,64,640]{2,1,0:T(8,128)(2,1)S(1)}, u32[]{:S(2)}, u32[]{:S(2)}) collective-permute-start(bf16[1,64,640]{2,1,0:T(8,128)(2,1)S(1)} %fusion.57), channel_id=1, source_target_pairs={{0,4},{1,5},{2,6},{3,7},{4,0},{5,1},{6,2},{7,3},{8,12},{9,13},{10,... | collective-permute-start | bytes 245768 | tf_op jit(solution)/shard_map/ppermute | solution.py:140
  84.3 2.7 %collective-permute-start.25 = (bf16[1,64,640]{2,1,0:T(8,128)(2,1)S(1)}, bf16[1,64,640]{2,1,0:T(8,128)(2,1)S(1)}, u32[]{:S(2)}, u32[]{:S(2)}) collective-permute-start(bf16[1,64,640]{2,1,0:T(8,128)(2,1)S(1)} %fusion.53), channel_id=1, source_target_pairs={{0,4},{1,5},{2,6},{3,7},{4,0},{5,1},{6,2},{7,3},{8,12},{9,13},{10,... | collective-permute-start | bytes 245768 | tf_op jit(solution)/shard_map/ppermute | solution.py:140
  87.0 2.0 %collective-permute-done.22 = bf16[1,64,640]{2,1,0:T(8,128)(2,1)S(1)} collective-permute-done((bf16[1,64,640]{2,1,0:T(8,128)(2,1)S(1)}, bf16[1,64,640]{2,1,0:T(8,128)(2,1)S(1)}, u32[]{:S(2)}, u32[]{:S(2)}) %collective-permute-start.22) | collective-permute-done | bytes 81952 | tf_op jit(solution)/shard_map/ppermute | solution.py:140
  89.0 2.1 %collective-permute-done.25 = bf16[1,64,640]{2,1,0:T(8,128)(2,1)S(1)} collective-permute-done((bf16[1,64,640]{2,1,0:T(8,128)(2,1)S(1)}, bf16[1,64,640]{2,1,0:T(8,128)(2,1)S(1)}, u32[]{:S(2)}, u32[]{:S(2)}) %collective-permute-start.25) | collective-permute-done | bytes 81952 | tf_op jit(solution)/shard_map/ppermute | solution.py:140
  (105 shorter events, 25.7 us)
Async XLA Ops:
  1.9 8.5 %collective-permute-start = (bf16[64,1280]{1,0:T(8,128)(2,1)}, bf16[64,1280]{1,0:T(8,128)(2,1)S(1)}, u32[]{:S(2)}, u32[]{:S(2)}) collective-permute-start(bf16[64,1280]{1,0:T(8,128)(2,1)} %get-tuple-element.15), channel_id=1, source_target_pairs={{0,8},{8,0},{16,24},{24,16},{1,9},{9,1},{17,25},{25,17},{2,10},{10... | collective-permute-start | bytes 491528 | tf_op jit(solution)/shard_map/ppermute | solution.py:140
  4.9 8.2 %collective-permute-start.1 = (bf16[64,1280]{1,0:T(8,128)(2,1)S(1)}, bf16[64,1280]{1,0:T(8,128)(2,1)S(1)}, u32[]{:S(2)}, u32[]{:S(2)}) collective-permute-start(bf16[64,1280]{1,0:T(8,128)(2,1)S(1)} %get-tuple-element.16), channel_id=1, source_target_pairs={{0,16},{8,24},{16,0},{24,8},{1,17},{9,25},{17,1},{25,9},{2,18},{10... | collective-permute-start | bytes 491528 | tf_op jit(solution)/shard_map/ppermute | solution.py:140
  6.4 7.7 %collective-permute-start.2 = (bf16[64,1280]{1,0:T(8,128)(2,1)S(1)}, bf16[64,1280]{1,0:T(8,128)(2,1)S(1)}, u32[]{:S(2)}, u32[]{:S(2)}) collective-permute-start(bf16[64,1280]{1,0:T(8,128)(2,1)S(1)} %get-tuple-element.17), channel_id=1, source_target_pairs={{0,24},{8,16},{16,8},{24,0},{1,25},{9,17},{17,9},{25,1},{2,26},{10... | collective-permute-start | bytes 491528 | tf_op jit(solution)/shard_map/ppermute | solution.py:140
  10.4 3.7 %collective-permute-start.3 = (bf16[64,1280]{1,0:T(8,128)(2,1)S(1)}, bf16[64,1280]{1,0:T(8,128)(2,1)S(1)}, u32[]{:S(2)}, u32[]{:S(2)}) collective-permute-start(bf16[64,1280]{1,0:T(8,128)(2,1)S(1)} %collective-permute-done), channel_id=1, source_target_pairs={{0,1},{1,0},{2,3},{3,2},{4,5},{5,4},{6,7},{7,6},{8,9},{9,8},{10,11... | collective-permute-start | bytes 491528 | tf_op jit(solution)/shard_map/ppermute | solution.py:140
  16.8 9.2 %collective-permute-start.8 = (bf16[64,1280]{1,0:T(8,128)(2,1)S(1)}, bf16[64,1280]{1,0:T(8,128)(2,1)S(1)}, u32[]{:S(2)}, u32[]{:S(2)}) collective-permute-start(bf16[64,1280]{1,0:T(8,128)(2,1)S(1)} %get-tuple-element.60), channel_id=1, source_target_pairs={{0,8},{8,0},{16,24},{24,16},{1,9},{9,1},{17,25},{25,17},{2,10},{10... | collective-permute-start | bytes 491528 | tf_op jit(solution)/shard_map/ppermute | solution.py:140
  18.3 8.1 %collective-permute-start.9 = (bf16[64,1280]{1,0:T(8,128)(2,1)S(1)}, bf16[64,1280]{1,0:T(8,128)(2,1)S(1)}, u32[]{:S(2)}, u32[]{:S(2)}) collective-permute-start(bf16[64,1280]{1,0:T(8,128)(2,1)S(1)} %get-tuple-element.60), channel_id=1, source_target_pairs={{0,16},{8,24},{16,0},{24,8},{1,17},{9,25},{17,1},{25,9},{2,18},{10... | collective-permute-start | bytes 491528 | tf_op jit(solution)/shard_map/ppermute | solution.py:140
  18.9 9.8 %collective-permute-start.10 = (bf16[64,1280]{1,0:T(8,128)(2,1)S(1)}, bf16[64,1280]{1,0:T(8,128)(2,1)S(1)}, u32[]{:S(2)}, u32[]{:S(2)}) collective-permute-start(bf16[64,1280]{1,0:T(8,128)(2,1)S(1)} %get-tuple-element.60), channel_id=1, source_target_pairs={{0,24},{8,16},{16,8},{24,0},{1,25},{9,17},{17,9},{25,1},{2,26},{10... | collective-permute-start | bytes 491528 | tf_op jit(solution)/shard_map/ppermute | solution.py:140
  23.0 16.2 %collective-permute-start.7 = (bf16[2,2,64,1024]{3,2,0,1:T(8,128)(2,1)S(1)}, bf16[2,2,64,1024]{3,2,0,1:T(8,128)(2,1)S(1)}, u32[]{:S(2)}, u32[]{:S(2)}) collective-permute-start(bf16[2,2,64,1024]{3,2,0,1:T(8,128)(2,1)S(1)} %fusion.11), channel_id=1, source_target_pairs={{0,16},{8,24},{16,0},{24,8},{1,17},{9,25},{17,1},{25,9},{2,18},{10... | collective-permute-start | bytes 1572872 | tf_op jit(solution)/shard_map/ppermute | solution.py:140
  24.8 14.4 %collective-permute-start.6 = (bf16[2,2,64,1024]{3,2,1,0:T(8,128)(2,1)S(1)}, bf16[2,2,64,1024]{3,2,1,0:T(8,128)(2,1)S(1)}, u32[]{:S(2)}, u32[]{:S(2)}) collective-permute-start(bf16[2,2,64,1024]{3,2,1,0:T(8,128)(2,1)S(1)} %fusion.8), channel_id=1, source_target_pairs={{0,8},{8,0},{16,24},{24,16},{1,9},{9,1},{17,25},{25,17},{2,10},{10... | collective-permute-start | bytes 1572872 | tf_op jit(solution)/shard_map/ppermute | solution.py:140
  39.2 7.1 %collective-permute-start.17 = (bf16[64,1280]{1,0:T(8,128)(2,1)S(1)}, bf16[64,1280]{1,0:T(8,128)(2,1)S(1)}, u32[]{:S(2)}, u32[]{:S(2)}) collective-permute-start(bf16[64,1280]{1,0:T(8,128)(2,1)S(1)} %get-tuple-element.29), channel_id=1, source_target_pairs={{0,8},{8,0},{16,24},{24,16},{1,9},{9,1},{17,25},{25,17},{2,10},{10... | collective-permute-start | bytes 491528 | tf_op jit(solution)/shard_map/ppermute | solution.py:140
  39.9 10.5 %collective-permute-start.18 = (bf16[64,1280]{1,0:T(8,128)(2,1)S(1)}, bf16[64,1280]{1,0:T(8,128)(2,1)S(1)}, u32[]{:S(2)}, u32[]{:S(2)}) collective-permute-start(bf16[64,1280]{1,0:T(8,128)(2,1)S(1)} %get-tuple-element.31), channel_id=1, source_target_pairs={{0,16},{8,24},{16,0},{24,8},{1,17},{9,25},{17,1},{25,9},{2,18},{10... | collective-permute-start | bytes 491528 | tf_op jit(solution)/shard_map/ppermute | solution.py:140
  41.6 8.7 %collective-permute-start.19 = (bf16[64,1280]{1,0:T(8,128)(2,1)S(1)}, bf16[64,1280]{1,0:T(8,128)(2,1)S(1)}, u32[]{:S(2)}, u32[]{:S(2)}) collective-permute-start(bf16[64,1280]{1,0:T(8,128)(2,1)S(1)} %get-tuple-element.30), channel_id=1, source_target_pairs={{0,24},{8,16},{16,8},{24,0},{1,25},{9,17},{17,9},{25,1},{2,26},{10... | collective-permute-start | bytes 491528 | tf_op jit(solution)/shard_map/ppermute | solution.py:140
  42.9 11.8 %collective-permute-start.11 = (bf16[2,1,64,1024]{3,2,0,1:T(8,128)(2,1)S(1)}, bf16[2,1,64,1024]{3,2,0,1:T(8,128)(2,1)S(1)}, u32[]{:S(2)}, u32[]{:S(2)}) collective-permute-start(bf16[2,1,64,1024]{3,2,0,1:T(8,128)(2,1)S(1)} %fusion.41), channel_id=1, source_target_pairs={{0,16},{8,24},{16,0},{24,8},{1,17},{9,25},{17,1},{25,9},{2,18},{10... | collective-permute-start | bytes 786440 | tf_op jit(solution)/shard_map/ppermute | solution.py:140
  43.8 10.9 %collective-permute-start.12 = (bf16[2,1,64,1024]{3,2,0,1:T(8,128)(2,1)S(1)}, bf16[2,1,64,1024]{3,2,0,1:T(8,128)(2,1)S(1)}, u32[]{:S(2)}, u32[]{:S(2)}) collective-permute-start(bf16[2,1,64,1024]{3,2,0,1:T(8,128)(2,1)S(1)} %fusion.42), channel_id=1, source_target_pairs={{0,8},{8,0},{16,24},{24,16},{1,9},{9,1},{17,25},{25,17},{2,10},{10... | collective-permute-start | bytes 786440 | tf_op jit(solution)/shard_map/ppermute | solution.py:140
  55.0 7.2 %collective-permute-start.15 = (bf16[2,1,64,512]{3,2,0,1:T(8,128)(2,1)S(1)}, bf16[2,1,64,512]{3,2,0,1:T(8,128)(2,1)S(1)}, u32[]{:S(2)}, u32[]{:S(2)}) collective-permute-start(bf16[2,1,64,512]{3,2,0,1:T(8,128)(2,1)S(1)} %get-tuple-element.55), channel_id=1, source_target_pairs={{0,8},{8,0},{16,24},{24,16},{1,9},{9,1},{17,25},{25,17},{2,10},{10... | collective-permute-start | bytes 393224 | tf_op jit(solution)/shard_map/ppermute | solution.py:140
  56.6 5.0 %collective-permute-start.13 = (bf16[2,1,64,512]{3,2,0,1:T(8,128)(2,1)S(1)}, bf16[2,1,64,512]{3,2,0,1:T(8,128)(2,1)S(1)}, u32[]{:S(2)}, u32[]{:S(2)}) collective-permute-start(bf16[2,1,64,512]{3,2,0,1:T(8,128)(2,1)S(1)} %get-tuple-element.56), channel_id=1, source_target_pairs={{0,16},{8,24},{16,0},{24,8},{1,17},{9,25},{17,1},{25,9},{2,18},{10... | collective-permute-start | bytes 393224 | tf_op jit(solution)/shard_map/ppermute | solution.py:140
  61.6 6.4 %collective-permute-start.14 = (bf16[2,2,64,512]{3,2,0,1:T(8,128)(2,1)S(1)}, bf16[2,2,64,512]{3,2,0,1:T(8,128)(2,1)S(1)}, u32[]{:S(2)}, u32[]{:S(2)}) collective-permute-start(bf16[2,2,64,512]{3,2,0,1:T(8,128)(2,1)S(1)} %get-tuple-element.58), channel_id=1, source_target_pairs={{0,8},{8,0},{16,24},{24,16},{1,9},{9,1},{17,25},{25,17},{2,10},{10... | collective-permute-start | bytes 786440 | tf_op jit(solution)/shard_map/ppermute | solution.py:140
  62.2 6.4 %collective-permute-start.16 = (bf16[2,2,64,512]{3,2,0,1:T(8,128)(2,1)S(1)}, bf16[2,2,64,512]{3,2,0,1:T(8,128)(2,1)S(1)}, u32[]{:S(2)}, u32[]{:S(2)}) collective-permute-start(bf16[2,2,64,512]{3,2,0,1:T(8,128)(2,1)S(1)} %get-tuple-element.52), channel_id=1, source_target_pairs={{0,16},{8,24},{16,0},{24,8},{1,17},{9,25},{17,1},{25,9},{2,18},{10... | collective-permute-start | bytes 786440 | tf_op jit(solution)/shard_map/ppermute | solution.py:140
  71.2 2.4 %collective-permute-start.20 = (bf16[256,640]{1,0:T(8,128)(2,1)S(1)}, bf16[256,640]{1,0:T(8,128)(2,1)S(1)}, u32[]{:S(2)}, u32[]{:S(2)}) collective-permute-start(bf16[256,640]{1,0:T(8,128)(2,1)S(1)} %fusion.14), channel_id=1, source_target_pairs={{0,1},{1,0},{2,3},{3,2},{4,5},{5,4},{6,7},{7,6},{8,9},{9,8},{10,11... | collective-permute-start | bytes 983048 | tf_op jit(solution)/shard_map/ppermute | solution.py:140
  72.4 2.9 %collective-permute-start.23 = (bf16[256,640]{1,0:T(8,128)(2,1)S(1)}, bf16[256,640]{1,0:T(8,128)(2,1)S(1)}, u32[]{:S(2)}, u32[]{:S(2)}) collective-permute-start(bf16[256,640]{1,0:T(8,128)(2,1)S(1)} %fusion.15), channel_id=1, source_target_pairs={{0,1},{1,0},{2,3},{3,2},{4,5},{5,4},{6,7},{7,6},{8,9},{9,8},{10,11... | collective-permute-start | bytes 983048 | tf_op jit(solution)/shard_map/ppermute | solution.py:140
  73.7 7.1 %collective-permute-start.21 = (bf16[2,64,640]{2,1,0:T(8,128)(2,1)S(1)}, bf16[2,64,640]{2,1,0:T(8,128)(2,1)S(1)}, u32[]{:S(2)}, u32[]{:S(2)}) collective-permute-start(bf16[2,64,640]{2,1,0:T(8,128)(2,1)S(1)} %pad_maximum_fusion.11), channel_id=1, source_target_pairs={{0,2},{1,3},{2,0},{3,1},{4,6},{5,7},{6,4},{7,5},{8,10},{9,11},{10,... | collective-permute-start | bytes 491528 | tf_op jit(solution)/shard_map/ppermute | solution.py:140
  75.5 8.8 %collective-permute-start.24 = (bf16[2,64,640]{2,1,0:T(8,128)(2,1)S(1)}, bf16[2,64,640]{2,1,0:T(8,128)(2,1)S(1)}, u32[]{:S(2)}, u32[]{:S(2)}) collective-permute-start(bf16[2,64,640]{2,1,0:T(8,128)(2,1)S(1)} %pad_maximum_fusion.12), channel_id=1, source_target_pairs={{0,2},{1,3},{2,0},{3,1},{4,6},{5,7},{6,4},{7,5},{8,10},{9,11},{10,... | collective-permute-start | bytes 491528 | tf_op jit(solution)/shard_map/ppermute | solution.py:140
  80.9 8.1 %collective-permute-start.22 = (bf16[1,64,640]{2,1,0:T(8,128)(2,1)S(1)}, bf16[1,64,640]{2,1,0:T(8,128)(2,1)S(1)}, u32[]{:S(2)}, u32[]{:S(2)}) collective-permute-start(bf16[1,64,640]{2,1,0:T(8,128)(2,1)S(1)} %fusion.57), channel_id=1, source_target_pairs={{0,4},{1,5},{2,6},{3,7},{4,0},{5,1},{6,2},{7,3},{8,12},{9,13},{10,... | collective-permute-start | bytes 245768 | tf_op jit(solution)/shard_map/ppermute | solution.py:140
  84.3 6.8 %collective-permute-start.25 = (bf16[1,64,640]{2,1,0:T(8,128)(2,1)S(1)}, bf16[1,64,640]{2,1,0:T(8,128)(2,1)S(1)}, u32[]{:S(2)}, u32[]{:S(2)}) collective-permute-start(bf16[1,64,640]{2,1,0:T(8,128)(2,1)S(1)} %fusion.53), channel_id=1, source_target_pairs={{0,4},{1,5},{2,6},{3,7},{4,0},{5,1},{6,2},{7,3},{8,12},{9,13},{10,... | collective-permute-start | bytes 245768 | tf_op jit(solution)/shard_map/ppermute | solution.py:140
  (13 other events, 87.2 us)
where the time goes:
time: 92.1 us; the launch traced here: 91.8 us
  waiting for transfers between devices  36.2 us (39%)
  starting transfers between devices  28.2 us (31%)
  Pallas kernels  10.7 us (12%)
  matrix products  7.41 us (8%)
  local copies, waits for them, and re-layouts  5.55 us (6%)
  other arithmetic  3.21 us (3%)
    ppermute x26, waiting for transfers between devices, swap(): return lax.ppermute(values, axis, [(i, i ^ step) for i in range(size)])  36.2 us
    ppermute x26, starting transfers between devices, swap(): return lax.ppermute(values, axis, [(i, i ^ step) for i in range(size)])  28.2 us
    pallas_call x1, Pallas kernels, expert(): pl.pallas_call(expert_kernel, out_shape=jax.ShapeDtypeStruct((slots, mode...  8.37 us
    dot_general x4, matrix products, dot(): out = jnp.dot(flat, weight, preferred_element_type=jnp.float32)  3.41 us
    pallas_call x1, Pallas kernels, slot_tables(): pl.pallas_call(functools.partial(table_kernel, n_row, half), out_shape=[j...  2.35 us
    dot_general x4, matrix products, combined(): part = jnp.dot(rows, down, preferred_element_type=jnp.float32)  2.3 us
    unnamed x22, local copies, waits for them, and re-layouts  2.2 us
    dynamic_slice x1, local copies, waits for them, and re-layouts, piece(): return lax.dynamic_slice(source, (top, block * width), (half, width))  1.92 us
  transfers between devices with their start and end apart: 26, of which 17 were waited for; matrix products, arithmetic and copies ran while one was open for 10% of the time, Pallas kernels for 12%

commit v1 on v0

--- a/solution.py
+++ b/solution.py
@@ -49,7 +49,7 @@
     return pl.pallas_call(
         functools.partial(table_kernel, n_row, half),
         out_shape=[
-            jax.ShapeDtypeStruct((slots, count), jnp.bfloat16),
+            pltpu.VMEM((slots, count), jnp.bfloat16),
             jax.ShapeDtypeStruct((2 * slots, count), jnp.bfloat16),
         ],
         in_specs=[smem, smem, vmem, vmem],
@@ -135,6 +135,32 @@
     )(scaled, w_gate, w_up, w_down)
 
 
+def act_kernel(gate_ref, gate_more, up_ref, up_more, first_ref, second_ref):
+    gate = gate_ref[...] + gate_more[...].astype(jnp.float32)
+    upper = up_ref[...] + up_more[...].astype(jnp.float32)
+    value = (gate / (1.0 + jnp.exp(-gate)) * upper).astype(jnp.bfloat16)
+    units = first_ref.shape[-1]
+    first_ref[...] = value[..., :units]
+    second_ref[...] = value[..., units:]
+
+
+def act(gate, gate_more, up, up_more):
+    shape = gate_more.shape[:-1] + (gate_more.shape[-1] // 2,)
+    vmem = pl.BlockSpec(shape, lambda i: (0, 0, 0, 0))
+    front = pl.BlockSpec(gate_more.shape, lambda i: (0, 0, 0, 0))
+    return pl.pallas_call(
+        act_kernel,
+        out_shape=[pltpu.VMEM(shape, jnp.bfloat16)] * 2,
+        grid=(1,),
+        in_specs=[front] * 4,
+        out_specs=[vmem] * 2,
+        name="act",
+        cost_estimate=pl.CostEstimate(
+            flops=8 * gate.size, bytes_accessed=16 * gate.size, transcendentals=gate.size
+        ),
+    )(gate, gate_more, up, up_more)
+
+
 def swap(values, axis, step):
     size = lax.axis_size(axis)
     return lax.ppermute(values, axis, [(i, i ^ step) for i in range(size)])
@@ -171,15 +197,15 @@
 
 
 def halve_rest(kept, came, order):
-    total = kept + came.astype(jnp.float32)
     done = [order[0]]
     for bit in order[1:]:
+        total = kept + came.astype(jnp.float32)
         at = bit - sum(1 for d in done if d < bit)
         away = bit_half(total, 1, at, 1).astype(jnp.bfloat16)
         came = swap(away, "row", 2**bit)
-        total = bit_half(total, 1, at, 0) + came.astype(jnp.float32)
+        kept = total if bit == order[-1] else bit_half(total, 1, at, 0)
         done.append(bit)
-    return total
+    return kept, came
 
 
 def spread(values, order):
@@ -255,10 +281,10 @@
         came = swap(leaving, "row", s)
         slot_total = slot_total + came.astype(jnp.float32)
 
-    shared_hidden = (jax.nn.silu(gate_sum) * up_sum).astype(jnp.bfloat16)
-    units = shared_hidden.shape[-1]
-    first = spread(shared_hidden[..., : units // 2], downward)
-    second = spread(shared_hidden[..., units // 2 :], upward)
+    units = shared_gate.shape[1]
+    first, second = act(*gate_sum, *up_sum)
+    first = spread(first, downward)
+    second = spread(second, upward)
     whole = jnp.concatenate([first, second], axis=-1)
     ordered = [lax.dynamic_index_in_dim(whole, row ^ chip ^ u, 1, False) for u in range(n_row)]
     outgoing = jnp.stack(ordered, axis=1).reshape(-1, units)
@@ -270,22 +296,25 @@
 
     lanes = width // 2
 
-    def combined(start, left):
+    def down(start):
         rows = outgoing[start : start + split]
-        down = shared_down[:, left : left + lanes]
-        part = jnp.dot(rows, down, preferred_element_type=jnp.float32)
-        put = placing[:, start : start + split]
-        return part + lax.dot_general(
-            put,
+        return jnp.dot(rows, shared_down, preferred_element_type=jnp.float32)
+
+    def placed(start, left):
+        return lax.dot_general(
+            placing[:, start : start + split],
             pair[:, left : left + lanes],
             (((0,), (0,)), ((), ())),
             preferred_element_type=jnp.float32,
         )
 
+    lefts = (0, lanes)
+    leaving, staying = down(split), down(0)
+    moved = [(leaving[:, i : i + lanes] + placed(split, i)).astype(jnp.bfloat16) for i in lefts]
+    moved = [swap(part, "col", 1) for part in moved]
     streams = []
-    for left in (0, lanes):
-        came = swap(combined(split, left).astype(jnp.bfloat16), "col", 1)
-        kept = lax.optimization_barrier(combined(0, left))
+    for left, came in zip(lefts, moved):
+        kept = lax.optimization_barrier(staying[:, left : left + lanes] + placed(0, left))
         total = (kept + came.astype(jnp.float32)).reshape(n_row, half, lanes)
         streams.append([total[u] for u in range(n_row)])
     for bit in range(bits):

time: 92.1 us -> 93.6 us (1.016)
  waiting for transfers between devices: 36.2 us -> 29.9 us
  local copies, waits for them, and re-layouts: 5.55 us -> 9.49 us
  other arithmetic: 3.21 us -> 5.62 us
  Pallas kernels: 10.7 us -> 12.3 us
    ppermute x26, waiting for transfers between devices: 36.2 us -> 29.9 us  [swap(): return lax.ppermute(values, axis, [(i, i ^ step) for i in range(size)])]
    add x0 -> x2, local copies, waits for them, and re-layouts: none -> 3.53 us  [halve_rest(): total = kept + came.astype(jnp.float32)]
    reshape x2 -> x1, other arithmetic: 0.26 us -> 1.9 us  [bit_half(): values.reshape(split)]
    pallas_call x1 -> x2, Pallas kernels: 2.35 us -> 3.89 us  [the longest x1 2.34 us: slot_tables(): pl.pallas_call(functools.partial(table_kernel, n_row, half), out_shape=[p...]
    unnamed x22 -> x26, local copies, waits for them, and re-layouts: 2.2 us -> 0.83 us
    convert_element_type x1, local copies, waits for them, and re-layouts: 0.07 us -> 1.22 us  [per_device(): leaving = columns(row ^ s).astype(jnp.bfloat16)]
    convert_element_type x1, other arithmetic: 0.09 us -> 1.07 us  [per_device(): high = slot_total.astype(jnp.bfloat16)]
    dot_general x8 -> x6, matrix products: 3.38 us -> 2.78 us  [the longest x2 1.68 us: down(): return jnp.dot(rows, shared_down, preferred_element_type=jnp.float32)]
  transfers between devices with their start and end apart: 26 -> 26, of which waited for: 17 -> 17; matrix products, arithmetic and copies ran while one was open for 10% -> 15% of each run, Pallas kernels for 12% -> 11%
where the time goes in v1:
time: 93.6 us; the launch traced here: 93.3 us
  waiting for transfers between devices  29.9 us (32%)
  starting transfers between devices  28.8 us (31%)
  Pallas kernels  12.3 us (13%)
  local copies, waits for them, and re-layouts  9.49 us (10%)
  matrix products  6.8 us (7%)
  other arithmetic  5.62 us (6%)
    ppermute x26, waiting for transfers between devices, swap(): return lax.ppermute(values, axis, [(i, i ^ step) for i in range(size)])  29.9 us
    ppermute x26, starting transfers between devices, swap(): return lax.ppermute(values, axis, [(i, i ^ step) for i in range(size)])  28.8 us
    pallas_call x1, Pallas kernels, expert(): pl.pallas_call(expert_kernel, out_shape=jax.ShapeDtypeStruct((slots, mode...  8.37 us
    add x2, local copies, waits for them, and re-layouts, halve_rest(): total = kept + came.astype(jnp.float32)  3.53 us
    dot_general x4, matrix products, dot(): out = jnp.dot(flat, weight, preferred_element_type=jnp.float32)  3.39 us
    pallas_call x1, Pallas kernels, slot_tables(): pl.pallas_call(functools.partial(table_kernel, n_row, half), out_shape=[p...  2.34 us
    dynamic_slice x1, local copies, waits for them, and re-layouts, piece(): return lax.dynamic_slice(source, (top, block * width), (half, width))  1.92 us
    reshape x1, other arithmetic, bit_half(): values.reshape(split)  1.9 us
  transfers between devices with their start and end apart: 26, of which 17 were waited for; matrix products, arithmetic and copies ran while one was open for 15% of the time, Pallas kernels for 11%

profile of v1, /device:TPU:0, one launch (start us, length us, event | category | flops | bytes accessed | tf_op | source)
XLA Modules:
  0.0 93.3 jit_solution(11860062698505762461)
XLA Ops:
  0.0 1.9 %fusion.63 = (bf16[64,1280]{1,0:T(8,128)(2,1)S(1)}, bf16[64,1280]{1,0:T(8,128)(2,1)S(1)}, bf16[64,1280]{1,0:T(8,128)(2,1)}) fusion(bf16[128,5120]{1,0:T(8,128)(2,1)} %param.11, s32[]{:T(128)S(6)} %select_n.43, s32[]{:T(128)S(6)} %select_n.46, s32[]{:T(128)S(6)} %select_n.45, s32[]{:T(128)S(6)} %select_n.44), kind=kLoop, calls=%fused_computation.120 | loop fusion | bytes 983056 | tf_op jit(solution)/shard_map/dynamic_slice | solution.py:244
  1.9 3.0 %collective-permute-start = (bf16[64,1280]{1,0:T(8,128)(2,1)}, bf16[64,1280]{1,0:T(8,128)(2,1)S(1)}, u32[]{:S(2)}, u32[]{:S(2)}) collective-permute-start(bf16[64,1280]{1,0:T(8,128)(2,1)} %get-tuple-element.17), channel_id=1, source_target_pairs={{0,8},{8,0},{16,24},{24,16},{1,9},{9,1},{17,25},{25,17},{2,10},{10... | collective-permute-start | bytes 491528 | tf_op jit(solution)/shard_map/ppermute | solution.py:166
  4.9 1.5 %collective-permute-start.1 = (bf16[64,1280]{1,0:T(8,128)(2,1)S(1)}, bf16[64,1280]{1,0:T(8,128)(2,1)S(1)}, u32[]{:S(2)}, u32[]{:S(2)}) collective-permute-start(bf16[64,1280]{1,0:T(8,128)(2,1)S(1)} %get-tuple-element.18), channel_id=1, source_target_pairs={{0,16},{8,24},{16,0},{24,8},{1,17},{9,25},{17,1},{25,9},{2,18},{10... | collective-permute-start | bytes 491528 | tf_op jit(solution)/shard_map/ppermute | solution.py:166
  7.1 2.3 %slot_tables.1 = (bf16[64,512]{1,0:T(8,128)(2,1)S(1)}, bf16[128,512]{1,0:T(8,128)(2,1)}) custom-call(s32[2]{0:T(128)} %pad_add_fusion.where, s32[2,8]{1,0:T(2,128)} %counts.1, s32[1,512]{1,0:T(1,128)} %bitcast.168, s32[1,512]{1,0:T(1,128)} %bitcast.169), custom_call_target="tpu_custom_call" | custom-call | flops 16777216 | bytes 4096 | tf_op jit(solution)/shard_map/slot_tables/pallas_call | solution.py:49
  10.5 2.6 %collective-permute-done.1 = bf16[64,1280]{1,0:T(8,128)(2,1)S(1)} collective-permute-done((bf16[64,1280]{1,0:T(8,128)(2,1)S(1)}, bf16[64,1280]{1,0:T(8,128)(2,1)S(1)}, u32[]{:S(2)}, u32[]{:S(2)}) %collective-permute-start.1) | collective-permute-done | bytes 163872 | tf_op jit(solution)/shard_map/ppermute | solution.py:166
  22.3 1.8 %collective-permute-start.7 = (bf16[2,2,64,1024]{3,2,0,1:T(8,128)(2,1)S(1)}, bf16[2,2,64,1024]{3,2,0,1:T(8,128)(2,1)S(1)}, u32[]{:S(2)}, u32[]{:S(2)}) collective-permute-start(bf16[2,2,64,1024]{3,2,0,1:T(8,128)(2,1)S(1)} %fusion.11), channel_id=1, source_target_pairs={{0,16},{8,24},{16,0},{24,8},{1,17},{9,25},{17,1},{25,9},{2,18},{10... | collective-permute-start | bytes 1572872 | tf_op jit(solution)/shard_map/ppermute | solution.py:166
  25.7 2.3 %collective-permute-done.10 = bf16[64,1280]{1,0:T(8,128)(2,1)S(1)} collective-permute-done((bf16[64,1280]{1,0:T(8,128)(2,1)S(1)}, bf16[64,1280]{1,0:T(8,128)(2,1)S(1)}, u32[]{:S(2)}, u32[]{:S(2)}) %collective-permute-start.10) | collective-permute-done | bytes 163872 | tf_op jit(solution)/shard_map/ppermute | solution.py:166
  28.6 8.4 %routed_expert.1 = f32[64,5120]{1,0:T(8,128)S(1)} custom-call(bf16[64,5120]{1,0:T(8,128)(2,1)S(1)} %multiply_convert_fusion.x_ref, bf16[1,5120,1024]{2,1,0:T(8,128)(2,1)S(1)} %bitcast.143, bf16[1,5120,1024]{2,1,0:T(8,128)(2,1)S(1)} %copy-done.1, bf16[1,1024,5120]{2,1,0:T(8,128)(2,1)} %down_hbm.1), custom_call_target="tpu_custom_call" | custom-call | flops 2013265920 | bytes 31457280 | tf_op jit(solution)/shard_map/routed_expert/pallas_call | solution.py:116
  37.0 1.5 %collective-permute-done.7 = bf16[2,2,64,1024]{3,2,0,1:T(8,128)(2,1)S(1)} collective-permute-done((bf16[2,2,64,1024]{3,2,0,1:T(8,128)(2,1)S(1)}, bf16[2,2,64,1024]{3,2,0,1:T(8,128)(2,1)S(1)}, u32[]{:S(2)}, u32[]{:S(2)}) %collective-permute-start.7) | collective-permute-done | bytes 524320 | tf_op jit(solution)/shard_map/ppermute | solution.py:166
  38.5 1.9 %convert_bitcast_fusion = (bf16[2,1,2,1,64,1024]{5,4,0,3,2,1:T(8,128)(2,1)S(1)}, f32[2,2,64,1024]{3,2,0,1:T(8,128)}, bf16[2,1,2,1,64,1024]{5,4,0,3,2,1:T(8,128)(2,1)S(1)}, f32[2,2,64,1024]{3,2,0,1:T(8,128)}) fusion(bf16[2,2,64,1024]{3,2,0,1:T(8,128)(2,1)S(1)} %collective-permute-done.7, f32[2,2,64,1024]{3,2,1,0:T(8,128)S(1)} %fusion, ...), kind=kLoop, calls=%fused_computation.56 | loop fusion | flops 1572864 | bytes 6291456 | tf_op jit(solution)/shard_map/reshape | solution.py:174
  41.9 1.7 %collective-permute-start.12 = (bf16[2,1,64,1024]{3,2,1,0:T(8,128)(2,1)}, bf16[2,1,64,1024]{3,2,1,0:T(8,128)(2,1)S(1)}, u32[]{:S(2)}, u32[]{:S(2)}) collective-permute-start(bf16[2,1,64,1024]{3,2,1,0:T(8,128)(2,1)} %slice_bitcast_fusion), channel_id=1, source_target_pairs={{0,8},{8,0},{16,24},{24,16},{1,9},{9,1},{17,25},{25,17},{2,10},{10... | collective-permute-start | bytes 786440 | tf_op jit(solution)/shard_map/ppermute | solution.py:166
  43.5 2.4 %copy.24.gate_ref = f32[2,2,64,1024]{3,2,1,0:T(8,128)} copy(f32[2,2,64,1024]{3,2,0,1:T(8,128)} %get-tuple-element.66) | data formatting | bytes 2097152 | tf_op jit(solution)/shard_map/add | solution.py:202
  47.1 1.6 %collective-permute-done.11.gate_more = bf16[2,1,64,1024]{3,2,1,0:T(8,128)(2,1)S(1)} collective-permute-done((bf16[2,1,64,1024]{3,2,1,0:T(8,128)(2,1)S(1)}, bf16[2,1,64,1024]{3,2,1,0:T(8,128)(2,1)S(1)}, u32[]{:S(2)}, u32[]{:S(2)}) %collective-permute-start.11) | collective-permute-done | bytes 262176 | tf_op jit(solution)/shard_map/ppermute | solution.py:166
  50.4 1.6 %act.1 = (bf16[2,1,64,512]{3,2,1,0:T(8,128)(2,1)S(1)}, bf16[2,1,64,512]{3,2,1,0:T(8,128)(2,1)S(1)}) custom-call(f32[2,2,64,1024]{3,2,1,0:T(8,128)} %copy.24.gate_ref, bf16[2,1,64,1024]{3,2,1,0:T(8,128)(2,1)} %copy-done.6, f32[2,2,64,1024]{3,2,1,0:T(8,128)} %copy.25.up_ref, bf16[2,1,64,1024]{3,2,1,0:T(8,128)(2,1)} %copy-done.7), custom_call_target="tpu_custom_call" | custom-call | flops 2097152 | bytes 4194304 | tf_op jit(solution)/shard_map/act/pallas_call | solution.py:151
  52.0 1.5 %collective-permute-start.15 = (bf16[2,1,64,512]{3,2,1,0:T(8,128)(2,1)S(1)}, bf16[2,1,64,512]{3,2,1,0:T(8,128)(2,1)S(1)}, u32[]{:S(2)}, u32[]{:S(2)}) collective-permute-start(bf16[2,1,64,512]{3,2,1,0:T(8,128)(2,1)S(1)} %get-tuple-element.24), channel_id=1, source_target_pairs={{0,8},{8,0},{16,24},{24,16},{1,9},{9,1},{17,25},{25,17},{2,10},{10... | collective-permute-start | bytes 393224 | tf_op jit(solution)/shard_map/ppermute | solution.py:166
  55.4 1.6 %collective-permute-start.17 = (bf16[64,1280]{1,0:T(8,128)(2,1)S(1)}, bf16[64,1280]{1,0:T(8,128)(2,1)S(1)}, u32[]{:S(2)}, u32[]{:S(2)}) collective-permute-start(bf16[64,1280]{1,0:T(8,128)(2,1)S(1)} %get-tuple-element.37), channel_id=1, source_target_pairs={{0,8},{8,0},{16,24},{24,16},{1,9},{9,1},{17,25},{25,17},{2,10},{10... | collective-permute-start | bytes 491528 | tf_op jit(solution)/shard_map/ppermute | solution.py:166
  57.4 1.6 %collective-permute-start.19 = (bf16[64,1280]{1,0:T(8,128)(2,1)S(1)}, bf16[64,1280]{1,0:T(8,128)(2,1)S(1)}, u32[]{:S(2)}, u32[]{:S(2)}) collective-permute-start(bf16[64,1280]{1,0:T(8,128)(2,1)S(1)} %get-tuple-element.38), channel_id=1, source_target_pairs={{0,24},{8,16},{16,8},{24,0},{1,25},{9,17},{17,9},{25,1},{2,26},{10... | collective-permute-start | bytes 491528 | tf_op jit(solution)/shard_map/ppermute | solution.py:166
  62.6 4.6 %collective-permute-done.18 = bf16[64,1280]{1,0:T(8,128)(2,1)S(1)} collective-permute-done((bf16[64,1280]{1,0:T(8,128)(2,1)S(1)}, bf16[64,1280]{1,0:T(8,128)(2,1)S(1)}, u32[]{:S(2)}, u32[]{:S(2)}) %collective-permute-start.18) | collective-permute-done | bytes 163872 | tf_op jit(solution)/shard_map/ppermute | solution.py:166
  75.2 1.6 %collective-permute-start.21 = (bf16[2,64,640]{2,1,0:T(8,128)(2,1)S(1)}, bf16[2,64,640]{2,1,0:T(8,128)(2,1)S(1)}, u32[]{:S(2)}, u32[]{:S(2)}) collective-permute-start(bf16[2,64,640]{2,1,0:T(8,128)(2,1)S(1)} %pad_maximum_fusion.11), channel_id=1, source_target_pairs={{0,2},{1,3},{2,0},{3,1},{4,6},{5,7},{6,4},{7,5},{8,10},{9,11},{10,... | collective-permute-start | bytes 491528 | tf_op jit(solution)/shard_map/ppermute | solution.py:166
  77.8 4.5 %collective-permute-done.21 = bf16[2,64,640]{2,1,0:T(8,128)(2,1)S(1)} collective-permute-done((bf16[2,64,640]{2,1,0:T(8,128)(2,1)S(1)}, bf16[2,64,640]{2,1,0:T(8,128)(2,1)S(1)}, u32[]{:S(2)}, u32[]{:S(2)}) %collective-permute-start.21) | collective-permute-done | bytes 163872 | tf_op jit(solution)/shard_map/ppermute | solution.py:166
  82.4 2.6 %collective-permute-start.22 = (bf16[1,64,640]{2,1,0:T(8,128)(2,1)S(1)}, bf16[1,64,640]{2,1,0:T(8,128)(2,1)S(1)}, u32[]{:S(2)}, u32[]{:S(2)}) collective-permute-start(bf16[1,64,640]{2,1,0:T(8,128)(2,1)S(1)} %fusion.45), channel_id=1, source_target_pairs={{0,4},{1,5},{2,6},{3,7},{4,0},{5,1},{6,2},{7,3},{8,12},{9,13},{10,... | collective-permute-start | bytes 245768 | tf_op jit(solution)/shard_map/ppermute | solution.py:166
  85.8 2.6 %collective-permute-start.25 = (bf16[1,64,640]{2,1,0:T(8,128)(2,1)S(1)}, bf16[1,64,640]{2,1,0:T(8,128)(2,1)S(1)}, u32[]{:S(2)}, u32[]{:S(2)}) collective-permute-start(bf16[1,64,640]{2,1,0:T(8,128)(2,1)S(1)} %fusion.41), channel_id=1, source_target_pairs={{0,4},{1,5},{2,6},{3,7},{4,0},{5,1},{6,2},{7,3},{8,12},{9,13},{10,... | collective-permute-start | bytes 245768 | tf_op jit(solution)/shard_map/ppermute | solution.py:166
  88.5 2.0 %collective-permute-done.22 = bf16[1,64,640]{2,1,0:T(8,128)(2,1)S(1)} collective-permute-done((bf16[1,64,640]{2,1,0:T(8,128)(2,1)S(1)}, bf16[1,64,640]{2,1,0:T(8,128)(2,1)S(1)}, u32[]{:S(2)}, u32[]{:S(2)}) %collective-permute-start.22) | collective-permute-done | bytes 81952 | tf_op jit(solution)/shard_map/ppermute | solution.py:166
  90.5 2.1 %collective-permute-done.25 = bf16[1,64,640]{2,1,0:T(8,128)(2,1)S(1)} collective-permute-done((bf16[1,64,640]{2,1,0:T(8,128)(2,1)S(1)}, bf16[1,64,640]{2,1,0:T(8,128)(2,1)S(1)}, u32[]{:S(2)}, u32[]{:S(2)}) %collective-permute-start.25) | collective-permute-done | bytes 81952 | tf_op jit(solution)/shard_map/ppermute | solution.py:166
  (107 shorter events, 33.5 us)
Async XLA Ops:
  1.9 8.5 %collective-permute-start = (bf16[64,1280]{1,0:T(8,128)(2,1)}, bf16[64,1280]{1,0:T(8,128)(2,1)S(1)}, u32[]{:S(2)}, u32[]{:S(2)}) collective-permute-start(bf16[64,1280]{1,0:T(8,128)(2,1)} %get-tuple-element.17), channel_id=1, source_target_pairs={{0,8},{8,0},{16,24},{24,16},{1,9},{9,1},{17,25},{25,17},{2,10},{10... | collective-permute-start | bytes 491528 | tf_op jit(solution)/shard_map/ppermute | solution.py:166
  4.9 8.2 %collective-permute-start.1 = (bf16[64,1280]{1,0:T(8,128)(2,1)S(1)}, bf16[64,1280]{1,0:T(8,128)(2,1)S(1)}, u32[]{:S(2)}, u32[]{:S(2)}) collective-permute-start(bf16[64,1280]{1,0:T(8,128)(2,1)S(1)} %get-tuple-element.18), channel_id=1, source_target_pairs={{0,16},{8,24},{16,0},{24,8},{1,17},{9,25},{17,1},{25,9},{2,18},{10... | collective-permute-start | bytes 491528 | tf_op jit(solution)/shard_map/ppermute | solution.py:166
  6.4 7.7 %collective-permute-start.2 = (bf16[64,1280]{1,0:T(8,128)(2,1)S(1)}, bf16[64,1280]{1,0:T(8,128)(2,1)S(1)}, u32[]{:S(2)}, u32[]{:S(2)}) collective-permute-start(bf16[64,1280]{1,0:T(8,128)(2,1)S(1)} %get-tuple-element.19), channel_id=1, source_target_pairs={{0,24},{8,16},{16,8},{24,0},{1,25},{9,17},{17,9},{25,1},{2,26},{10... | collective-permute-start | bytes 491528 | tf_op jit(solution)/shard_map/ppermute | solution.py:166
  10.4 3.7 %collective-permute-start.3 = (bf16[64,1280]{1,0:T(8,128)(2,1)S(1)}, bf16[64,1280]{1,0:T(8,128)(2,1)S(1)}, u32[]{:S(2)}, u32[]{:S(2)}) collective-permute-start(bf16[64,1280]{1,0:T(8,128)(2,1)S(1)} %collective-permute-done), channel_id=1, source_target_pairs={{0,1},{1,0},{2,3},{3,2},{4,5},{5,4},{6,7},{7,6},{8,9},{9,8},{10,11... | collective-permute-start | bytes 491528 | tf_op jit(solution)/shard_map/ppermute | solution.py:166
  16.1 9.2 %collective-permute-start.8 = (bf16[64,1280]{1,0:T(8,128)(2,1)S(1)}, bf16[64,1280]{1,0:T(8,128)(2,1)S(1)}, u32[]{:S(2)}, u32[]{:S(2)}) collective-permute-start(bf16[64,1280]{1,0:T(8,128)(2,1)S(1)} %get-tuple-element.64), channel_id=1, source_target_pairs={{0,8},{8,0},{16,24},{24,16},{1,9},{9,1},{17,25},{25,17},{2,10},{10... | collective-permute-start | bytes 491528 | tf_op jit(solution)/shard_map/ppermute | solution.py:166
  17.6 8.1 %collective-permute-start.9 = (bf16[64,1280]{1,0:T(8,128)(2,1)S(1)}, bf16[64,1280]{1,0:T(8,128)(2,1)S(1)}, u32[]{:S(2)}, u32[]{:S(2)}) collective-permute-start(bf16[64,1280]{1,0:T(8,128)(2,1)S(1)} %get-tuple-element.64), channel_id=1, source_target_pairs={{0,16},{8,24},{16,0},{24,8},{1,17},{9,25},{17,1},{25,9},{2,18},{10... | collective-permute-start | bytes 491528 | tf_op jit(solution)/shard_map/ppermute | solution.py:166
  18.2 9.8 %collective-permute-start.10 = (bf16[64,1280]{1,0:T(8,128)(2,1)S(1)}, bf16[64,1280]{1,0:T(8,128)(2,1)S(1)}, u32[]{:S(2)}, u32[]{:S(2)}) collective-permute-start(bf16[64,1280]{1,0:T(8,128)(2,1)S(1)} %get-tuple-element.64), channel_id=1, source_target_pairs={{0,24},{8,16},{16,8},{24,0},{1,25},{9,17},{17,9},{25,1},{2,26},{10... | collective-permute-start | bytes 491528 | tf_op jit(solution)/shard_map/ppermute | solution.py:166
  22.3 16.2 %collective-permute-start.7 = (bf16[2,2,64,1024]{3,2,0,1:T(8,128)(2,1)S(1)}, bf16[2,2,64,1024]{3,2,0,1:T(8,128)(2,1)S(1)}, u32[]{:S(2)}, u32[]{:S(2)}) collective-permute-start(bf16[2,2,64,1024]{3,2,0,1:T(8,128)(2,1)S(1)} %fusion.11), channel_id=1, source_target_pairs={{0,16},{8,24},{16,0},{24,8},{1,17},{9,25},{17,1},{25,9},{2,18},{10... | collective-permute-start | bytes 1572872 | tf_op jit(solution)/shard_map/ppermute | solution.py:166
  24.1 14.4 %collective-permute-start.6 = (bf16[2,2,64,1024]{3,2,0,1:T(8,128)(2,1)S(1)}, bf16[2,2,64,1024]{3,2,0,1:T(8,128)(2,1)S(1)}, u32[]{:S(2)}, u32[]{:S(2)}) collective-permute-start(bf16[2,2,64,1024]{3,2,0,1:T(8,128)(2,1)S(1)} %fusion.8), channel_id=1, source_target_pairs={{0,8},{8,0},{16,24},{24,16},{1,9},{9,1},{17,25},{25,17},{2,10},{10... | collective-permute-start | bytes 1572872 | tf_op jit(solution)/shard_map/ppermute | solution.py:166
  40.4 8.3 %collective-permute-start.11 = (bf16[2,1,64,1024]{3,2,1,0:T(8,128)(2,1)S(1)}, bf16[2,1,64,1024]{3,2,1,0:T(8,128)(2,1)S(1)}, u32[]{:S(2)}, u32[]{:S(2)}) collective-permute-start(bf16[2,1,64,1024]{3,2,1,0:T(8,128)(2,1)S(1)} %slice_bitcast_fusion.1), channel_id=1, source_target_pairs={{0,16},{8,24},{16,0},{24,8},{1,17},{9,25},{17,1},{25,9},{2,18},{10... | collective-permute-start | bytes 786440 | tf_op jit(solution)/shard_map/ppermute | solution.py:166
  41.9 7.8 %collective-permute-start.12 = (bf16[2,1,64,1024]{3,2,1,0:T(8,128)(2,1)}, bf16[2,1,64,1024]{3,2,1,0:T(8,128)(2,1)S(1)}, u32[]{:S(2)}, u32[]{:S(2)}) collective-permute-start(bf16[2,1,64,1024]{3,2,1,0:T(8,128)(2,1)} %slice_bitcast_fusion), channel_id=1, source_target_pairs={{0,8},{8,0},{16,24},{24,16},{1,9},{9,1},{17,25},{25,17},{2,10},{10... | collective-permute-start | bytes 786440 | tf_op jit(solution)/shard_map/ppermute | solution.py:166
  52.0 7.0 %collective-permute-start.15 = (bf16[2,1,64,512]{3,2,1,0:T(8,128)(2,1)S(1)}, bf16[2,1,64,512]{3,2,1,0:T(8,128)(2,1)S(1)}, u32[]{:S(2)}, u32[]{:S(2)}) collective-permute-start(bf16[2,1,64,512]{3,2,1,0:T(8,128)(2,1)S(1)} %get-tuple-element.24), channel_id=1, source_target_pairs={{0,8},{8,0},{16,24},{24,16},{1,9},{9,1},{17,25},{25,17},{2,10},{10... | collective-permute-start | bytes 393224 | tf_op jit(solution)/shard_map/ppermute | solution.py:166
  53.5 6.9 %collective-permute-start.13 = (bf16[2,1,64,512]{3,2,1,0:T(8,128)(2,1)S(1)}, bf16[2,1,64,512]{3,2,1,0:T(8,128)(2,1)S(1)}, u32[]{:S(2)}, u32[]{:S(2)}) collective-permute-start(bf16[2,1,64,512]{3,2,1,0:T(8,128)(2,1)S(1)} %get-tuple-element.23), channel_id=1, source_target_pairs={{0,16},{8,24},{16,0},{24,8},{1,17},{9,25},{17,1},{25,9},{2,18},{10... | collective-permute-start | bytes 393224 | tf_op jit(solution)/shard_map/ppermute | solution.py:166
  55.4 7.1 %collective-permute-start.17 = (bf16[64,1280]{1,0:T(8,128)(2,1)S(1)}, bf16[64,1280]{1,0:T(8,128)(2,1)S(1)}, u32[]{:S(2)}, u32[]{:S(2)}) collective-permute-start(bf16[64,1280]{1,0:T(8,128)(2,1)S(1)} %get-tuple-element.37), channel_id=1, source_target_pairs={{0,8},{8,0},{16,24},{24,16},{1,9},{9,1},{17,25},{25,17},{2,10},{10... | collective-permute-start | bytes 491528 | tf_op jit(solution)/shard_map/ppermute | solution.py:166
  57.0 10.2 %collective-permute-start.18 = (bf16[64,1280]{1,0:T(8,128)(2,1)S(1)}, bf16[64,1280]{1,0:T(8,128)(2,1)S(1)}, u32[]{:S(2)}, u32[]{:S(2)}) collective-permute-start(bf16[64,1280]{1,0:T(8,128)(2,1)S(1)} %get-tuple-element.39), channel_id=1, source_target_pairs={{0,16},{8,24},{16,0},{24,8},{1,17},{9,25},{17,1},{25,9},{2,18},{10... | collective-permute-start | bytes 491528 | tf_op jit(solution)/shard_map/ppermute | solution.py:166
  57.4 9.8 %collective-permute-start.19 = (bf16[64,1280]{1,0:T(8,128)(2,1)S(1)}, bf16[64,1280]{1,0:T(8,128)(2,1)S(1)}, u32[]{:S(2)}, u32[]{:S(2)}) collective-permute-start(bf16[64,1280]{1,0:T(8,128)(2,1)S(1)} %get-tuple-element.38), channel_id=1, source_target_pairs={{0,24},{8,16},{16,8},{24,0},{1,25},{9,17},{17,9},{25,1},{2,26},{10... | collective-permute-start | bytes 491528 | tf_op jit(solution)/shard_map/ppermute | solution.py:166
  59.0 12.1 %collective-permute-start.16 = (bf16[2,2,64,512]{3,2,0,1:T(8,128)(2,1)S(1)}, bf16[2,2,64,512]{3,2,0,1:T(8,128)(2,1)S(1)}, u32[]{:S(2)}, u32[]{:S(2)}) collective-permute-start(bf16[2,2,64,512]{3,2,0,1:T(8,128)(2,1)S(1)} %get-tuple-element.60), channel_id=1, source_target_pairs={{0,16},{8,24},{16,0},{24,8},{1,17},{9,25},{17,1},{25,9},{2,18},{10... | collective-permute-start | bytes 786440 | tf_op jit(solution)/shard_map/ppermute | solution.py:166
  60.5 9.3 %collective-permute-start.14 = (bf16[2,2,64,512]{3,2,0,1:T(8,128)(2,1)S(1)}, bf16[2,2,64,512]{3,2,0,1:T(8,128)(2,1)S(1)}, u32[]{:S(2)}, u32[]{:S(2)}) collective-permute-start(bf16[2,2,64,512]{3,2,0,1:T(8,128)(2,1)S(1)} %get-tuple-element.62), channel_id=1, source_target_pairs={{0,8},{8,0},{16,24},{24,16},{1,9},{9,1},{17,25},{25,17},{2,10},{10... | collective-permute-start | bytes 786440 | tf_op jit(solution)/shard_map/ppermute | solution.py:166
  72.8 2.3 %collective-permute-start.20 = (bf16[256,640]{1,0:T(8,128)(2,1)S(1)}, bf16[256,640]{1,0:T(8,128)(2,1)S(1)}, u32[]{:S(2)}, u32[]{:S(2)}) collective-permute-start(bf16[256,640]{1,0:T(8,128)(2,1)S(1)} %fusion.14), channel_id=1, source_target_pairs={{0,1},{1,0},{2,3},{3,2},{4,5},{5,4},{6,7},{7,6},{8,9},{9,8},{10,11... | collective-permute-start | bytes 983048 | tf_op jit(solution)/shard_map/ppermute | solution.py:166
  74.2 2.6 %collective-permute-start.23 = (bf16[256,640]{1,0:T(8,128)(2,1)S(1)}, bf16[256,640]{1,0:T(8,128)(2,1)S(1)}, u32[]{:S(2)}, u32[]{:S(2)}) collective-permute-start(bf16[256,640]{1,0:T(8,128)(2,1)S(1)} %fusion.15), channel_id=1, source_target_pairs={{0,1},{1,0},{2,3},{3,2},{4,5},{5,4},{6,7},{7,6},{8,9},{9,8},{10,11... | collective-permute-start | bytes 983048 | tf_op jit(solution)/shard_map/ppermute | solution.py:166
  75.2 7.1 %collective-permute-start.21 = (bf16[2,64,640]{2,1,0:T(8,128)(2,1)S(1)}, bf16[2,64,640]{2,1,0:T(8,128)(2,1)S(1)}, u32[]{:S(2)}, u32[]{:S(2)}) collective-permute-start(bf16[2,64,640]{2,1,0:T(8,128)(2,1)S(1)} %pad_maximum_fusion.11), channel_id=1, source_target_pairs={{0,2},{1,3},{2,0},{3,1},{4,6},{5,7},{6,4},{7,5},{8,10},{9,11},{10,... | collective-permute-start | bytes 491528 | tf_op jit(solution)/shard_map/ppermute | solution.py:166
  77.0 8.8 %collective-permute-start.24 = (bf16[2,64,640]{2,1,0:T(8,128)(2,1)S(1)}, bf16[2,64,640]{2,1,0:T(8,128)(2,1)S(1)}, u32[]{:S(2)}, u32[]{:S(2)}) collective-permute-start(bf16[2,64,640]{2,1,0:T(8,128)(2,1)S(1)} %pad_maximum_fusion.12), channel_id=1, source_target_pairs={{0,2},{1,3},{2,0},{3,1},{4,6},{5,7},{6,4},{7,5},{8,10},{9,11},{10,... | collective-permute-start | bytes 491528 | tf_op jit(solution)/shard_map/ppermute | solution.py:166
  82.4 8.1 %collective-permute-start.22 = (bf16[1,64,640]{2,1,0:T(8,128)(2,1)S(1)}, bf16[1,64,640]{2,1,0:T(8,128)(2,1)S(1)}, u32[]{:S(2)}, u32[]{:S(2)}) collective-permute-start(bf16[1,64,640]{2,1,0:T(8,128)(2,1)S(1)} %fusion.45), channel_id=1, source_target_pairs={{0,4},{1,5},{2,6},{3,7},{4,0},{5,1},{6,2},{7,3},{8,12},{9,13},{10,... | collective-permute-start | bytes 245768 | tf_op jit(solution)/shard_map/ppermute | solution.py:166
  85.8 6.8 %collective-permute-start.25 = (bf16[1,64,640]{2,1,0:T(8,128)(2,1)S(1)}, bf16[1,64,640]{2,1,0:T(8,128)(2,1)S(1)}, u32[]{:S(2)}, u32[]{:S(2)}) collective-permute-start(bf16[1,64,640]{2,1,0:T(8,128)(2,1)S(1)} %fusion.41), channel_id=1, source_target_pairs={{0,4},{1,5},{2,6},{3,7},{4,0},{5,1},{6,2},{7,3},{8,12},{9,13},{10,... | collective-permute-start | bytes 245768 | tf_op jit(solution)/shard_map/ppermute | solution.py:166
  (15 other events, 125.5 us)
